TPU v7x, 128 devices: a whole 4x4x4 slice. The times are simulated.
128 devices in a mesh: ctx: 32 (over y, z, x_lo), seq: 2 (over core), fsdp: 2 (over x_hi).
Axes of the slice: x: 4 (x_hi: 2, x_lo: 2; x = x_hi * 2 + x_lo), y: 4, z: 4, core: 2. Of those that a mesh axis runs over, the one named last changes fastest.
Arguments:
- tokens: bfloat16 [4, 4096, 768], P(('seq', 'fsdp'), 'ctx'), may hold values from -6 to 6
- cotangent: bfloat16 [4, 4096, 768], P(('seq', 'fsdp'), 'ctx'), may hold values from -6 to 6
- w_query: bfloat16 [768, 768], P('fsdp'), may hold values from -0.21875 to 0.21875
- w_key: bfloat16 [768, 768], P('fsdp'), may hold values from -0.21875 to 0.21875
- w_value: bfloat16 [768, 768], P('fsdp'), may hold values from -0.21875 to 0.21875
- w_output: bfloat16 [768, 768], P('fsdp'), may hold values from -6 to 6
- b_query: bfloat16 [768], P('fsdp'), may hold values from -1.5 to 1.5
- b_value: bfloat16 [768], P('fsdp'), may hold values from -0.15625 to 0.15625
- b_output: bfloat16 [768], P('fsdp'), may hold values from -1.5 to 1.5
- first_gain: bfloat16 [768], P('fsdp'), may hold values from 0.5 to 1.5
- first_shift: bfloat16 [768], P('fsdp'), may hold values from -1.5 to 1.5
- w_inner: bfloat16 [768, 3072], P('fsdp'), may hold values from -0.21875 to 0.21875
- b_inner: bfloat16 [3072], P('fsdp'), may hold values from -1.5 to 1.5
- w_outer: bfloat16 [3072, 768], P('fsdp'), may hold values from -0.109375 to 0.109375
- b_outer: bfloat16 [768], P('fsdp'), may hold values from -1.5 to 1.5
- second_gain: bfloat16 [768], P('fsdp'), may hold values from 0.5 to 1.5
- second_shift: bfloat16 [768], P('fsdp'), may hold values from -1.5 to 1.5
Outputs:
- layer_out: bfloat16 [4, 4096, 768], P(('seq', 'fsdp'), 'ctx')
- tokens_grad: float32 [4, 4096, 768], P(('seq', 'fsdp'), 'ctx')
- w_query_grad: float32 [768, 768], P('fsdp')
- w_key_grad: float32 [768, 768], P('fsdp')
- w_value_grad: float32 [768, 768], P('fsdp')
- w_output_grad: float32 [768, 768], P('fsdp')
- b_query_grad: float32 [768], P('fsdp')
- b_value_grad: float32 [768], P('fsdp')
- b_output_grad: float32 [768], P('fsdp')
- first_gain_grad: float32 [768], P('fsdp')
- first_shift_grad: float32 [768], P('fsdp')
- w_inner_grad: float32 [768, 3072], P('fsdp')
- b_inner_grad: float32 [3072], P('fsdp')
- w_outer_grad: float32 [3072, 768], P('fsdp')
- b_outer_grad: float32 [768], P('fsdp')
- second_gain_grad: float32 [768], P('fsdp')
- second_shift_grad: float32 [768], P('fsdp')
All inputs are finite; a program needn't handle non-finite values.
Results may differ from a plain program's by a relative error of at most 0.022.
Values may be sent and summed in bfloat16 or wider, within the bound.
A program may use at most 192 MiB of HBM per device.

v0:
```python
import functools
import jax
import jax.numpy as jnp
from jax import lax
from jax.sharding import PartitionSpec as P

HEADS = 12
HEAD_DIM = 64
epsilon = 1e-12


def product(left, right):
    return jnp.dot(left, right, preferred_element_type=jnp.float32)


def product_left(left, right):
    return lax.dot_general(
        left, right, (((0,), (0,)), ((), ())), preferred_element_type=jnp.float32
    )


def product_right(left, right):
    return lax.dot_general(
        left, right, (((1,), (1,)), ((), ())), preferred_element_type=jnp.float32
    )


def layer_norm(hidden, gain, shift):
    centred = hidden - jnp.mean(hidden, axis=-1, keepdims=True)
    inverse = lax.rsqrt(jnp.mean(centred * centred, axis=-1, keepdims=True) + epsilon)
    normal = centred * inverse
    return (normal * gain + shift, normal, inverse)


def norm_back(grad, normal, inverse, gain):
    scaled = grad * gain
    centre = jnp.mean(scaled, axis=-1, keepdims=True)
    along = jnp.mean(scaled * normal, axis=-1, keepdims=True)
    return inverse * (scaled - centre - normal * along)


def group_slice(array, index):
    columns = 2 * HEAD_DIM
    piece = lax.dynamic_slice_in_dim(array, index * columns, columns, 2)
    return piece.reshape(piece.shape[0], piece.shape[1], 2, HEAD_DIM)


def scores_of(query, keys):
    return jnp.einsum(
        "sqhd,skhd->shqk", query, keys, preferred_element_type=jnp.float32
    ) * HEAD_DIM ** (-0.5)


def flatten_group(array):
    return array.reshape(array.shape[0], array.shape[1], 2 * HEAD_DIM)


def to_rows(stacked):
    groups, seqs, count, columns = stacked.shape
    return stacked.transpose(1, 2, 0, 3).reshape(seqs * count, groups * columns)


def local(
    tokens,
    cotangent,
    w_query,
    w_key,
    w_value,
    w_output,
    b_query,
    b_value,
    b_output,
    first_gain,
    first_shift,
    w_inner,
    b_inner,
    w_outer,
    b_outer,
    second_gain,
    second_shift,
):
    seqs, block, width = tokens.shape
    rows = seqs * block
    indices = jnp.arange(HEADS // 2)
    scale = HEAD_DIM ** (-0.5)
    w_query, w_key, w_value, w_output, b_query, b_value, b_output, first_gain, first_shift = (
        lax.all_gather(w_query, "fsdp", axis=0, tiled=True),
        lax.all_gather(w_key, "fsdp", axis=0, tiled=True),
        lax.all_gather(w_value, "fsdp", axis=0, tiled=True),
        lax.all_gather(w_output, "fsdp", axis=0, tiled=True),
        lax.all_gather(b_query, "fsdp", axis=0, tiled=True),
        lax.all_gather(b_value, "fsdp", axis=0, tiled=True),
        lax.all_gather(b_output, "fsdp", axis=0, tiled=True),
        lax.all_gather(first_gain, "fsdp", axis=0, tiled=True),
        lax.all_gather(first_shift, "fsdp", axis=0, tiled=True),
    )
    flat = tokens.reshape(rows, width)
    query = (product(flat, w_query) + b_query).astype(jnp.bfloat16).reshape(seqs, block, width)
    keys = product(flat, w_key).astype(jnp.bfloat16).reshape(seqs, block, width)
    values = (product(flat, w_value) + b_value).astype(jnp.bfloat16).reshape(seqs, block, width)
    keys_all, values_all = (
        lax.all_gather(keys, "ctx", axis=1, tiled=True),
        lax.all_gather(values, "ctx", axis=1, tiled=True),
    )

    def forward_group(index):
        scores = scores_of(group_slice(query, index), group_slice(keys_all, index))
        top = jnp.max(scores, axis=-1, keepdims=True)
        weights = jnp.exp(scores - top)
        total = jnp.sum(weights, axis=-1, keepdims=True)
        probs = (weights / total).astype(jnp.bfloat16)
        mixed = jnp.einsum(
            "shqk,skhd->sqhd",
            probs,
            group_slice(values_all, index),
            preferred_element_type=jnp.float32,
        )
        return (flatten_group(mixed), (top + jnp.log(total))[..., 0])

    mixed, logsum = lax.map(forward_group, indices)
    attended = to_rows(mixed).astype(jnp.bfloat16)
    first_in = flat.astype(jnp.float32) + product(attended, w_output) + b_output
    normed, first_normal, first_inverse = layer_norm(first_in, first_gain, first_shift)
    normed_low = normed.astype(jnp.bfloat16)
    w_inner, b_inner, w_outer, b_outer, second_gain, second_shift = (
        lax.all_gather(w_inner, "fsdp", axis=0, tiled=True),
        lax.all_gather(b_inner, "fsdp", axis=0, tiled=True),
        lax.all_gather(w_outer, "fsdp", axis=0, tiled=True),
        lax.all_gather(b_outer, "fsdp", axis=0, tiled=True),
        lax.all_gather(second_gain, "fsdp", axis=0, tiled=True),
        lax.all_gather(second_shift, "fsdp", axis=0, tiled=True),
    )
    gelu_exact = functools.partial(jax.nn.gelu, approximate=False)
    inner = product(normed_low, w_inner) + b_inner
    active = gelu_exact(inner).astype(jnp.bfloat16)
    second_in = normed + product(active, w_outer) + b_outer
    layer_out, second_normal, second_inverse = layer_norm(second_in, second_gain, second_shift)
    grad_out = cotangent.reshape(rows, width).astype(jnp.float32)
    second_scale = jnp.sum(grad_out * second_normal, axis=0)
    second_offset = jnp.sum(grad_out, axis=0)
    grad_second = norm_back(grad_out, second_normal, second_inverse, second_gain)
    outer_low = grad_second.astype(jnp.bfloat16)
    outer_matrix = product_left(active, outer_low)
    outer_bias = jnp.sum(outer_low.astype(jnp.float32), axis=0)
    slope = jax.vjp(gelu_exact, inner)[1](product_right(outer_low, w_outer))[0]
    inner_low = slope.astype(jnp.bfloat16)
    inner_matrix = product_left(normed_low, inner_low)
    inner_bias = jnp.sum(inner_low.astype(jnp.float32), axis=0)
    grad_normed = grad_second + product_right(inner_low, w_inner)
    first_scale = jnp.sum(grad_normed * first_normal, axis=0)
    first_offset = jnp.sum(grad_normed, axis=0)
    grad_first = norm_back(grad_normed, first_normal, first_inverse, first_gain)
    branch_low = grad_first.astype(jnp.bfloat16)
    output_matrix = product_left(attended, branch_low)
    output_bias = jnp.sum(branch_low.astype(jnp.float32), axis=0)
    upstream = product_right(branch_low, w_output).astype(jnp.bfloat16).reshape(seqs, block, width)

    def backward_group(pair):
        index, group_logsum = pair
        query_part = group_slice(query, index)
        keys_part = group_slice(keys_all, index)
        values_part = group_slice(values_all, index)
        upstream_part = group_slice(upstream, index)
        probs = jnp.exp(scores_of(query_part, keys_part) - group_logsum[..., None])
        prob_grads = jnp.einsum(
            "sqhd,skhd->shqk", upstream_part, values_part, preferred_element_type=jnp.float32
        )
        row_dot = jnp.sum(probs * prob_grads, axis=-1, keepdims=True)
        score_low = (probs * (prob_grads - row_dot)).astype(jnp.bfloat16)
        query_grad = (
            jnp.einsum("shqk,skhd->sqhd", score_low, keys_part, preferred_element_type=jnp.float32)
            * scale
        )
        key_grad = (
            jnp.einsum("shqk,sqhd->skhd", score_low, query_part, preferred_element_type=jnp.float32)
            * scale
        )
        value_grad = jnp.einsum(
            "shqk,sqhd->skhd",
            probs.astype(jnp.bfloat16),
            upstream_part,
            preferred_element_type=jnp.float32,
        )
        return (flatten_group(query_grad), flatten_group(key_grad), flatten_group(value_grad))

    query_grads, key_terms, value_terms = lax.map(backward_group, (indices, logsum))
    key_grads, value_grads = (
        lax.psum_scatter(
            key_terms.astype(jnp.bfloat16), "ctx", scatter_dimension=2, tiled=True
        ).astype(jnp.float32),
        lax.psum_scatter(
            value_terms.astype(jnp.bfloat16), "ctx", scatter_dimension=2, tiled=True
        ).astype(jnp.float32),
    )
    query_low = to_rows(query_grads).astype(jnp.bfloat16)
    key_low = to_rows(key_grads).astype(jnp.bfloat16)
    value_low = to_rows(value_grads).astype(jnp.bfloat16)
    query_matrix = product_left(flat, query_low)
    query_bias = jnp.sum(query_low.astype(jnp.float32), axis=0)
    keys_matrix = product_left(flat, key_low)
    value_matrix = product_left(flat, value_low)
    value_bias = jnp.sum(value_low.astype(jnp.float32), axis=0)
    tokens_grad = (
        grad_first
        + product_right(query_low, w_query)
        + product_right(key_low, w_key)
        + product_right(value_low, w_value)
    )
    (
        query_matrix,
        keys_matrix,
        value_matrix,
        output_matrix,
        query_bias,
        value_bias,
        output_bias,
        first_scale,
        first_offset,
        inner_matrix,
        inner_bias,
        outer_matrix,
        outer_bias,
        second_scale,
        second_offset,
    ) = (
        lax.psum_scatter(
            query_matrix.astype(jnp.bfloat16), "fsdp", scatter_dimension=0, tiled=True
        ).astype(jnp.float32),
        lax.psum_scatter(
            keys_matrix.astype(jnp.bfloat16), "fsdp", scatter_dimension=0, tiled=True
        ).astype(jnp.float32),
        lax.psum_scatter(
            value_matrix.astype(jnp.bfloat16), "fsdp", scatter_dimension=0, tiled=True
        ).astype(jnp.float32),
        lax.psum_scatter(
            output_matrix.astype(jnp.bfloat16), "fsdp", scatter_dimension=0, tiled=True
        ).astype(jnp.float32),
        lax.psum_scatter(
            query_bias.astype(jnp.bfloat16), "fsdp", scatter_dimension=0, tiled=True
        ).astype(jnp.float32),
        lax.psum_scatter(
            value_bias.astype(jnp.bfloat16), "fsdp", scatter_dimension=0, tiled=True
        ).astype(jnp.float32),
        lax.psum_scatter(
            output_bias.astype(jnp.bfloat16), "fsdp", scatter_dimension=0, tiled=True
        ).astype(jnp.float32),
        lax.psum_scatter(
            first_scale.astype(jnp.bfloat16), "fsdp", scatter_dimension=0, tiled=True
        ).astype(jnp.float32),
        lax.psum_scatter(
            first_offset.astype(jnp.bfloat16), "fsdp", scatter_dimension=0, tiled=True
        ).astype(jnp.float32),
        lax.psum_scatter(
            inner_matrix.astype(jnp.bfloat16), "fsdp", scatter_dimension=0, tiled=True
        ).astype(jnp.float32),
        lax.psum_scatter(
            inner_bias.astype(jnp.bfloat16), "fsdp", scatter_dimension=0, tiled=True
        ).astype(jnp.float32),
        lax.psum_scatter(
            outer_matrix.astype(jnp.bfloat16), "fsdp", scatter_dimension=0, tiled=True
        ).astype(jnp.float32),
        lax.psum_scatter(
            outer_bias.astype(jnp.bfloat16), "fsdp", scatter_dimension=0, tiled=True
        ).astype(jnp.float32),
        lax.psum_scatter(
            second_scale.astype(jnp.bfloat16), "fsdp", scatter_dimension=0, tiled=True
        ).astype(jnp.float32),
        lax.psum_scatter(
            second_offset.astype(jnp.bfloat16), "fsdp", scatter_dimension=0, tiled=True
        ).astype(jnp.float32),
    )
    finals = lax.psum(
        (
            query_matrix,
            keys_matrix,
            value_matrix,
            output_matrix,
            query_bias,
            value_bias,
            output_bias,
            first_scale,
            first_offset,
            inner_matrix,
            inner_bias,
            outer_matrix,
            outer_bias,
            second_scale,
            second_offset,
        ),
        ("ctx", "seq"),
    )
    return (
        layer_out.astype(jnp.bfloat16).reshape(seqs, block, width),
        tokens_grad.reshape(seqs, block, width),
    ) + tuple(finals)


def solution(mesh):
    return jax.shard_map(
        local,
        mesh=mesh,
        in_specs=(
            P(("seq", "fsdp"), "ctx", None),
            P(("seq", "fsdp"), "ctx", None),
            P("fsdp", None),
            P("fsdp", None),
            P("fsdp", None),
            P("fsdp", None),
            P("fsdp"),
            P("fsdp"),
            P("fsdp"),
            P("fsdp"),
            P("fsdp"),
            P("fsdp", None),
            P("fsdp"),
            P("fsdp", None),
            P("fsdp"),
            P("fsdp"),
            P("fsdp"),
        ),
        out_specs=(
            P(("seq", "fsdp"), "ctx", None),
            P(("seq", "fsdp"), "ctx", None),
            P("fsdp", None),
            P("fsdp", None),
            P("fsdp", None),
            P("fsdp", None),
            P("fsdp"),
            P("fsdp"),
            P("fsdp"),
            P("fsdp"),
            P("fsdp"),
            P("fsdp", None),
            P("fsdp"),
            P("fsdp", None),
            P("fsdp"),
            P("fsdp"),
            P("fsdp"),
        ),
        check_vma=False,
    )
```

profile of v0, /device:TPU:0, one launch (start us, length us, event | category | flops | bytes accessed | tf_op | source)
XLA Modules:
  0.0 1809.2 jit_solution(1213545254661435694)
XLA Ops:
  15.4 23.6 %all-gather.20.cloned.1.call-done = bf16[768,768]{1,0:T(8,128)(2,1)} async-done(((bf16[384,768]{1,0:T(8,128)(2,1)}), bf16[768,768]{1,0:T(8,128)(2,1)}) %all-gather.20.cloned.1.call-update) | async-done | bytes 1179664 | tf_op jit(solution)/shard_map/all_gather | solution.py:89
  41.3 25.6 %all-gather.24.cloned.1.call-done = bf16[768,768]{1,0:T(8,128)(2,1)} async-done(((bf16[384,768]{1,0:T(8,128)(2,1)}), bf16[768,768]{1,0:T(8,128)(2,1)}) %all-gather.24.cloned.1.call-update) | async-done | bytes 1179664 | tf_op jit(solution)/shard_map/all_gather | solution.py:88
  120.5 150.1 %all-gather.32.cloned.1.call-done = bf16[4096,768]{1,0:T(8,128)(2,1)} async-done(((bf16[128,768]{1,0:T(8,128)(2,1)}), bf16[4096,768]{1,0:T(8,128)(2,1)}) %all-gather.32.cloned.1.call-update) | async-done | bytes 6291472 | tf_op jit(solution)/shard_map/all_gather | solution.py:103
  270.5 8.7 copy.44
  279.2 166.5 %all-gather.34.cloned.1.call-done = bf16[4096,768]{1,0:T(8,128)(2,1)} async-done(((bf16[128,768]{1,0:T(8,128)(2,1)}), bf16[4096,768]{1,0:T(8,128)(2,1)}) %all-gather.34.cloned.1.call-update) | async-done | bytes 6291472 | tf_op jit(solution)/shard_map/all_gather | solution.py:102
  445.8 8.6 copy.46
  454.4 33.8 %while.26 = (s32[]{:T(128)}, bf16[6,1,128,128]{2,3,1,0:T(8,128)(2,1)S(1)}, f32[6,1,2,128]{3,2,1,0:T(2,128)S(1)}, s32[6]{0:T(128)S(1)}, bf16[1,4096,768]{1,2,0:T(...) while((s32[]{:T(128)}, ...), condition=%wide.region_3.4_spmd, body=%wide.region_0.3_spmd.sunk | while | flops 275775232 | bytes 19079360 | solution.py:120
  490.3 49.7 %all-gather.28.cloned.1.call-done = bf16[768,3072]{1,0:T(8,128)(2,1)} async-done(((bf16[384,3072]{1,0:T(8,128)(2,1)}), bf16[768,3072]{1,0:T(8,128)(2,1)}) %all-gather.28.cloned.1.call-update) | async-done | bytes 4718608 | tf_op jit(solution)/shard_map/all_gather | solution.py:126
  548.4 59.5 %all-gather.30.cloned.1.call-done = bf16[3072,768]{1,0:T(8,128)(2,1)} async-done(((bf16[1536,768]{1,0:T(8,128)(2,1)}), bf16[3072,768]{1,0:T(8,128)(2,1)}) %all-gather.30.cloned.1.call-update) | async-done | bytes 4718608 | tf_op jit(solution)/shard_map/all_gather | solution.py:128
  619.1 72.0 %while.27 = (s32[]{:T(128)}, bf16[6,1,128,128]{2,3,1,0:T(8,128)(2,1)S(1)}, bf16[6,1,4096,128]{2,3,1,0:T(8,128)(2,1)}, bf16[6,1,4096,128]{2,3,1,0:T(8,128)(2,1)},...) while((s32[]{:T(128)}, ...), condition=%wide.region_14.15_spmd, body=%wide.region_12.14_spmd.sunk | while | flops 680558336 | bytes 47093020 | solution.py:186
  691.1 27.8 %copy.54 = bf16[6,1,4096,128]{3,1,0,2:T(2,128)(2,1)} copy(bf16[6,1,4096,128]{2,3,1,0:T(8,128)(2,1)} %get-tuple-element.112) | data formatting | bytes 12582912
  718.9 110.1 %bitcast_reduce_fusion.1 = bf16[4096,6,128]{2,1,0:T(8,128)(2,1)} fusion(bf16[6,1,4096,128]{3,1,0,2:T(2,128)(2,1)} %copy.54), kind=kLoop, calls=%fused_computation.29 | loop fusion | bytes 12582912
  836.8 27.9 %copy.56 = bf16[6,1,4096,128]{3,1,0,2:T(2,128)(2,1)} copy(bf16[6,1,4096,128]{2,3,1,0:T(8,128)(2,1)} %get-tuple-element.113) | data formatting | bytes 12582912
  864.6 110.0 %bitcast_reduce_fusion = bf16[4096,6,128]{2,1,0:T(8,128)(2,1)} fusion(bf16[6,1,4096,128]{3,1,0,2:T(2,128)(2,1)} %copy.56), kind=kLoop, calls=%fused_computation.28 | loop fusion | bytes 12582912
  995.5 21.0 %reduce-scatter.25.cloned.1.call-done = bf16[128,768]{1,0:T(8,128)(2,1)} async-done(((bf16[4096,768]{1,0:T(8,128)(2,1)}), bf16[128,768]{1,0:T(8,128)(2,1)}) %reduce-scatter.25.cloned.1.call-update) | async-done | bytes 196624
  1020.3 176.3 %reduce-scatter.27.cloned.1.call-done = bf16[128,768]{1,0:T(8,128)(2,1)} async-done(((bf16[4096,768]{1,0:T(8,128)(2,1)}), bf16[128,768]{1,0:T(8,128)(2,1)}) %reduce-scatter.27.cloned.1.call-update) | async-done | bytes 196624
  1203.8 18.1 reduce-scatter.29.cloned.1.call-done
  1223.3 26.8 %reduce-scatter.19.cloned.1.call-done = bf16[384,768]{1,0:T(8,128)(2,1)} async-done(((bf16[768,768]{1,0:T(8,128)(2,1)}), bf16[384,768]{1,0:T(8,128)(2,1)}) %reduce-scatter.19.cloned.1.call-update) | async-done | bytes 589840 | tf_op jit(solution)/shard_map/reduce_scatter | solution.py:235
  1250.1 66.5 %reduce-scatter.21.cloned.1.call-done = bf16[384,3072]{1,0:T(8,128)(2,1)} async-done(((bf16[768,3072]{1,0:T(8,128)(2,1)}), bf16[384,3072]{1,0:T(8,128)(2,1)}) %reduce-scatter.21.cloned.1.call-update) | async-done | bytes 2359312 | tf_op jit(solution)/shard_map/reduce_scatter | solution.py:253
  1316.5 66.5 %reduce-scatter.23.cloned.1.call-done = bf16[1536,768]{1,0:T(8,128)(2,1)} async-done(((bf16[3072,768]{1,0:T(8,128)(2,1)}), bf16[1536,768]{1,0:T(8,128)(2,1)}) %reduce-scatter.23.cloned.1.call-update) | async-done | bytes 2359312 | tf_op jit(solution)/shard_map/reduce_scatter | solution.py:259
  1383.2 8.6 all-reduce.10
  1395.3 15.8 reduce-scatter.31.cloned.1.call-done
  1412.4 26.8 %reduce-scatter.33.cloned.1.call-done = bf16[384,768]{1,0:T(8,128)(2,1)} async-done(((bf16[768,768]{1,0:T(8,128)(2,1)}), bf16[384,768]{1,0:T(8,128)(2,1)}) %reduce-scatter.33.cloned.1.call-update) | async-done | bytes 589840
  1440.6 356.2 %all-reduce.12 = (f32[384,768]{0,1:T(8,128)}, f32[384,768]{0,1:T(8,128)}, f32[384,768]{0,1:T(8,128)S(1)}, f32[384,768]{1,0:T(8,128)}, f32[384]{0:T(512)}, /*inde...) all-reduce(bf16[384,768]{0,1:T(8,128)(2,1)S(1)} %copy.59, ...), channel_id=1, replica_groups=mesh['ctx'=32,'seq'=2,'fsdp'=2] {'ctx','seq'}, use_global_device_ids=true, to_apply=%region_18.19 | all-reduce | flops 3543552 | bytes 21270528 | tf_op jit(solution)/shard_map/psum | solution.py:272
  (359 shorter events, 233.4 us)
Async XLA Ops:
  7.2 31.8 %copy-start = (bf16[1,128,768]{2,1,0:T(8,128)(2,1)S(1)}, bf16[1,128,768]{2,1,0:T(8,128)(2,1)}, u32[]{:S(2)}) copy-start(bf16[1,128,768]{2,1,0:T(8,128)(2,1)} %param.21) | copy-start | bytes 589828
  7.2 31.8 %all-gather.20.cloned.1.call-start = ((), (), s32[]{:S(2)}) async-start(), calls=%async_computation.8 | async-start | bytes 1769472 | tf_op jit(solution)/shard_map/all_gather | solution.py:89
  7.9 59.0 %all-gather.24.cloned.1.call-start = ((), (), s32[]{:S(2)}) async-start(), calls=%async_computation.10 | async-start | bytes 1769472 | tf_op jit(solution)/shard_map/all_gather | solution.py:88
  8.7 110.0 %all-gather.22.cloned.1.call-start = ((), (), s32[]{:S(2)}) async-start(), calls=%async_computation.9 | async-start | bytes 1769472 | tf_op jit(solution)/shard_map/all_gather | solution.py:87
  9.4 261.1 %all-gather.32.cloned.1.call-start = ((), (), s32[]{:S(2)}) async-start(), calls=%async_computation.17 | async-start | bytes 6488064 | tf_op jit(solution)/shard_map/all_gather | solution.py:103
  41.3 404.5 %all-gather.34.cloned.1.call-start = ((), (), s32[]{:S(2)}) async-start(), calls=%async_computation.18 | async-start | bytes 6488064 | tf_op jit(solution)/shard_map/all_gather | solution.py:102
  69.2 419.0 %all-gather.26.cloned.1.call-start = ((), (), s32[]{:S(2)}) async-start(), calls=%async_computation.11 | async-start | bytes 1769472 | tf_op jit(solution)/shard_map/all_gather | solution.py:90
  69.8 470.2 %all-gather.28.cloned.1.call-start = ((), (), s32[]{:S(2)}) async-start(), calls=%async_computation.12 | async-start | bytes 7077888 | tf_op jit(solution)/shard_map/all_gather | solution.py:126
  70.6 30.3 %copy-start.22 = (bf16[384]{0:T(512)(128)(2,1)S(1)}, bf16[384]{0:T(512)(128)(2,1)}, u32[]{:S(2)}) copy-start(bf16[384]{0:T(512)(128)(2,1)} %param.30) | copy-start | bytes 2308
  70.6 36.2 %copy-start.23 = (bf16[384]{0:T(512)(128)(2,1)S(1)}, bf16[384]{0:T(512)(128)(2,1)}, u32[]{:S(2)}) copy-start(bf16[384]{0:T(512)(128)(2,1)} %param.36) | copy-start | bytes 2308
  70.6 42.1 %copy-start.24 = (bf16[384]{0:T(512)(128)(2,1)S(1)}, bf16[384]{0:T(512)(128)(2,1)}, u32[]{:S(2)}) copy-start(bf16[384]{0:T(512)(128)(2,1)} %param.37) | copy-start | bytes 2308
  70.7 537.2 %all-gather.30.cloned.1.call-start = ((), (), s32[]{:S(2)}) async-start(), calls=%async_computation.13 | async-start | bytes 7077888 | tf_op jit(solution)/shard_map/all_gather | solution.py:128
  71.4 945.1 %reduce-scatter.25.cloned.1.call-start = ((), (), s32[]{:S(2)}) async-start(), calls=%async_computation.19 | async-start | bytes 6488064
  488.2 60.2 %copy-start.7 = (bf16[6,1,128,128]{2,3,1,0:T(8,128)(2,1)}, bf16[6,1,128,128]{2,3,1,0:T(8,128)(2,1)S(1)}, u32[]{:S(2)}) copy-start(bf16[6,1,128,128]{2,3,1,0:T(8,128)(2,1)S(1)} %get-tuple-element.109) | copy-start | bytes 589828
  836.7 359.9 %reduce-scatter.27.cloned.1.call-start = ((), (), s32[]{:S(2)}) async-start(), calls=%async_computation.20 | async-start | bytes 6488064
  982.3 239.6 %reduce-scatter.29.cloned.1.call-start = ((), (), s32[]{:S(2)}) async-start(), calls=%async_computation.21 | async-start | bytes 1769472
  986.3 263.8 %reduce-scatter.19.cloned.1.call-start = ((), (), s32[]{:S(2)}) async-start(), calls=%async_computation.14 | async-start | bytes 1769472 | tf_op jit(solution)/shard_map/reduce_scatter | solution.py:235
  988.0 328.5 %reduce-scatter.21.cloned.1.call-start = ((), (), s32[]{:S(2)}) async-start(), calls=%async_computation.15 | async-start | bytes 7077888 | tf_op jit(solution)/shard_map/reduce_scatter | solution.py:253
  991.8 391.2 %reduce-scatter.23.cloned.1.call-start = ((), (), s32[]{:S(2)}) async-start(), calls=%async_computation.16 | async-start | bytes 7077888 | tf_op jit(solution)/shard_map/reduce_scatter | solution.py:259
  995.5 415.5 %reduce-scatter.31.cloned.1.call-start = ((), (), s32[]{:S(2)}) async-start(), calls=%async_computation.22 | async-start | bytes 1769472
  1020.3 418.9 %reduce-scatter.33.cloned.1.call-start = ((), (), s32[]{:S(2)}) async-start(), calls=%async_computation.23 | async-start | bytes 1769472
  1202.5 189.9 %copy-start.2 = (bf16[768,768]{1,0:T(8,128)(2,1)S(1)}, bf16[768,768]{1,0:T(8,128)(2,1)}, u32[]{:S(2)}) copy-start(bf16[768,768]{1,0:T(8,128)(2,1)} %all-gather.24.cloned.1.call-done) | copy-start | bytes 3538948
  1203.8 188.7 %copy-start.10 = (bf16[6,1,128,128]{2,3,1,0:T(8,128)(2,1)S(1)}, bf16[6,1,128,128]{2,3,1,0:T(8,128)(2,1)}, u32[]{:S(2)}) copy-start(bf16[6,1,128,128]{2,3,1,0:T(8,128)(2,1)} %copy-done.9) | copy-start | bytes 589828
  1203.8 190.2 %copy-start.1 = (bf16[768,768]{1,0:T(8,128)(2,1)S(1)}, bf16[768,768]{1,0:T(8,128)(2,1)}, u32[]{:S(2)}) copy-start(bf16[768,768]{1,0:T(8,128)(2,1)} %all-gather.20.cloned.1.call-done) | copy-start | bytes 3538948
  (34 other events, 125.0 us)
Sparse Core Ops, SparseCore 0:
  9.7 29.2 all-gather.19
  40.6 26.2 all-gather.23
  68.6 26.3 all-gather.21
  97.1 173.4 all-gather.31
  272.6 173.1 all-gather.33
  447.3 24.7 all-gather.25
  473.7 66.2 all-gather.27
  541.6 66.1 all-gather.29
  836.8 179.6 reduce-scatter.24
  1018.8 177.7 reduce-scatter.26
  1199.5 22.3 reduce-scatter.28
  1224.8 25.2 reduce-scatter.18
  1253.0 63.4 reduce-scatter.20
  1319.5 63.4 reduce-scatter.22
  1385.8 25.2 reduce-scatter.30
  1413.9 25.2 reduce-scatter.32
where the time goes:
time: 1820 us; the launch traced here: 1810 us
  waiting for transfers between devices  897 us (49%)
  blocking collectives  417 us (23%)
  local copies, waits for them, and re-layouts  382 us (21%)
  matrix products  74.2 us (4%)
    psum x1, blocking collectives, local(): lax.psum((query_matrix, keys_matrix, value_matrix, output_matrix, query_b...  356 us
    unnamed x89, local copies, waits for them, and re-layouts  312 us
    unnamed x21, waiting for transfers between devices  262 us
    all_gather x1, waiting for transfers between devices, local(): lax.all_gather(keys, 'ctx', axis=1, tiled=True)  167 us
    all_gather x1, waiting for transfers between devices, local(): lax.all_gather(values, 'ctx', axis=1, tiled=True)  150 us
    reduce_scatter x1, waiting for transfers between devices, local(): lax.psum_scatter(outer_matrix.astype(jnp.bfloat16), 'fsdp', scatter_dimen...  66.5 us
    reduce_scatter x1, waiting for transfers between devices, local(): lax.psum_scatter(inner_matrix.astype(jnp.bfloat16), 'fsdp', scatter_dimen...  66.5 us
    all_gather x1, waiting for transfers between devices, local(): lax.all_gather(w_outer, 'fsdp', axis=0, tiled=True)  59.5 us
  transfers between devices with their start and end apart: 16, of which 14 were waited for; matrix products, arithmetic and copies ran while one was open for 13% of the time, Pallas kernels for 0%

commit v1 on v0

--- a/solution.py
+++ b/solution.py
@@ -7,6 +7,15 @@
 HEADS = 12
 HEAD_DIM = 64
 epsilon = 1e-12
+
+
+def replace_domain(packet, array_dim):
+    return jnp.concatenate(
+        jax.lax.all_to_all(
+            jnp.stack(tuple((packet for _ in range(jax.lax.axis_size("ctx"))))), "ctx", 0, 0
+        ),
+        axis=array_dim,
+    )
 
 
 def product(left, right):
@@ -100,7 +109,7 @@
     values = (product(flat, w_value) + b_value).astype(jnp.bfloat16).reshape(seqs, block, width)
     keys_all, values_all = (
         lax.all_gather(keys, "ctx", axis=1, tiled=True),
-        lax.all_gather(values, "ctx", axis=1, tiled=True),
+        replace_domain(values, 1),
     )
 
     def forward_group(index):

time: 1820 us -> 1700 us (0.934)
  waiting for transfers between devices: 897 us -> 649 us
  blocking collectives: 417 us -> 530 us
    all_gather x1 -> x0, waiting for transfers between devices: 150 us -> none  [local(): lax.all_gather(values, 'ctx', axis=1, tiled=True)]
    all_gather x1, blocking collectives: 5.83 us -> 118 us  [local(): lax.all_gather(b_outer, 'fsdp', axis=0, tiled=True)]
    all_gather x1, waiting for transfers between devices: 167 us -> 69.2 us  [local(): lax.all_gather(keys, 'ctx', axis=1, tiled=True)]
    unnamed x21 -> x20, waiting for transfers between devices: 262 us -> 262 us
    unnamed x89 -> x91, local copies, waits for them, and re-layouts: 312 us -> 312 us
  transfers between devices with their start and end apart: 16 -> 16, of which waited for: 14 -> 13; matrix products, arithmetic and copies ran while one was open for 13% -> 15% of each run, Pallas kernels for 0% -> 0%
where the time goes in v1:
time: 1700 us; the launch traced here: 1690 us
  waiting for transfers between devices  649 us (38%)
  blocking collectives  530 us (31%)
  local copies, waits for them, and re-layouts  395 us (23%)
  matrix products  73.7 us (4%)
    psum x1, blocking collectives, local(): lax.psum((query_matrix, keys_matrix, value_matrix, output_matrix, query_b...  356 us
    unnamed x91, local copies, waits for them, and re-layouts  312 us
    unnamed x20, waiting for transfers between devices  262 us
    all_gather x1, blocking collectives, local(): lax.all_gather(b_outer, 'fsdp', axis=0, tiled=True)  118 us
    all_gather x1, waiting for transfers between devices, local(): lax.all_gather(keys, 'ctx', axis=1, tiled=True)  69.2 us
    reduce_scatter x1, waiting for transfers between devices, local(): lax.psum_scatter(outer_matrix.astype(jnp.bfloat16), 'fsdp', scatter_dimen...  66.6 us
    reduce_scatter x1, waiting for transfers between devices, local(): lax.psum_scatter(inner_matrix.astype(jnp.bfloat16), 'fsdp', scatter_dimen...  66.3 us
    all_gather x1, waiting for transfers between devices, local(): lax.all_gather(w_outer, 'fsdp', axis=0, tiled=True)  59.5 us
  transfers between devices with their start and end apart: 16, of which 13 were waited for; matrix products, arithmetic and copies ran while one was open for 15% of the time, Pallas kernels for 0%

profile of v1, /device:TPU:0, one launch (start us, length us, event | category | flops | bytes accessed | tf_op | source)
XLA Modules:
  0.0 1694.4 jit_solution(1911568244248455209)
XLA Ops:
  9.5 29.5 %all-gather.22.cloned.1.call-done = bf16[768,768]{1,0:T(8,128)(2,1)} async-done(((bf16[384,768]{1,0:T(8,128)(2,1)}), bf16[768,768]{1,0:T(8,128)(2,1)}) %all-gather.22.cloned.1.call-update) | async-done | bytes 1179664 | tf_op jit(solution)/shard_map/all_gather | solution.py:97
  47.8 19.2 %all-gather.18.cloned.1.call-done = bf16[768,768]{1,0:T(8,128)(2,1)} async-done(((bf16[384,768]{1,0:T(8,128)(2,1)}), bf16[768,768]{1,0:T(8,128)(2,1)}) %all-gather.18.cloned.1.call-update) | async-done | bytes 1179664 | tf_op jit(solution)/shard_map/all_gather | solution.py:98
  81.7 118.3 %all-gather.7 = bf16[2,1,384]{2,1,0:T(2,128)(2,1)S(1)} all-gather(bf16[1,1,384]{2,1,0:T(2,128)(2,1)S(1)} %reshape.272), channel_id=1, replica_groups=mesh['ctx'=32,'seq'=2,'fsdp'=2] {'fsdp'}, dimensions={0}, use_global_device_ids=true | all-gather | bytes 2304 | tf_op jit(solution)/shard_map/all_gather | solution.py:138
  243.3 8.6 copy.53
  251.9 8.8 copy.54
  260.7 69.2 %all-gather.30.cloned.1.call-done = bf16[4096,768]{1,0:T(8,128)(2,1)} async-done(((bf16[128,768]{1,0:T(8,128)(2,1)}), bf16[4096,768]{1,0:T(8,128)(2,1)}) %all-gather.30.cloned.1.call-update) | async-done | bytes 6291472 | tf_op jit(solution)/shard_map/all_gather | solution.py:111
  329.8 8.6 copy.56
  338.5 33.6 %while.26 = (s32[]{:T(128)}, bf16[6,1,128,128]{2,3,1,0:T(8,128)(2,1)S(1)}, f32[6,1,2,128]{3,2,1,0:T(2,128)S(1)}, s32[6]{0:T(128)S(1)}, bf16[1,4096,768]{1,2,0:T(...) while((s32[]{:T(128)}, ...), condition=%wide.region_3.4_spmd, body=%wide.region_0.3_spmd.sunk | while | flops 275775232 | bytes 19079360 | solution.py:129
  374.3 49.1 %all-gather.26.cloned.1.call-done = bf16[768,3072]{1,0:T(8,128)(2,1)} async-done(((bf16[384,3072]{1,0:T(8,128)(2,1)}), bf16[768,3072]{1,0:T(8,128)(2,1)}) %all-gather.26.cloned.1.call-update) | async-done | bytes 4718608 | tf_op jit(solution)/shard_map/all_gather | solution.py:135
  431.7 59.5 %all-gather.28.cloned.1.call-done = bf16[3072,768]{1,0:T(8,128)(2,1)} async-done(((bf16[1536,768]{1,0:T(8,128)(2,1)}), bf16[3072,768]{1,0:T(8,128)(2,1)}) %all-gather.28.cloned.1.call-update) | async-done | bytes 4718608 | tf_op jit(solution)/shard_map/all_gather | solution.py:137
  502.5 71.9 %while.27 = (s32[]{:T(128)}, bf16[6,1,128,128]{2,3,1,0:T(8,128)(2,1)S(1)}, bf16[6,1,4096,128]{2,3,1,0:T(8,128)(2,1)}, bf16[6,1,4096,128]{2,3,1,0:T(8,128)(2,1)},...) while((s32[]{:T(128)}, ...), condition=%wide.region_14.15_spmd, body=%wide.region_12.14_spmd.sunk | while | flops 680558336 | bytes 47093020 | solution.py:195
  574.4 27.9 %copy.64 = bf16[6,1,4096,128]{3,1,0,2:T(2,128)(2,1)} copy(bf16[6,1,4096,128]{2,3,1,0:T(8,128)(2,1)} %get-tuple-element.112) | data formatting | bytes 12582912
  602.2 110.3 %bitcast_reduce_fusion.1 = bf16[4096,6,128]{2,1,0:T(8,128)(2,1)} fusion(bf16[6,1,4096,128]{3,1,0,2:T(2,128)(2,1)} %copy.64), kind=kLoop, calls=%fused_computation.29 | loop fusion | bytes 12582912
  720.3 27.9 %copy.66 = bf16[6,1,4096,128]{3,1,0,2:T(2,128)(2,1)} copy(bf16[6,1,4096,128]{2,3,1,0:T(8,128)(2,1)} %get-tuple-element.113) | data formatting | bytes 12582912
  748.2 109.9 %bitcast_reduce_fusion = bf16[4096,6,128]{2,1,0:T(8,128)(2,1)} fusion(bf16[6,1,4096,128]{3,1,0,2:T(2,128)(2,1)} %copy.66), kind=kLoop, calls=%fused_computation.28 | loop fusion | bytes 12582912
  879.0 21.7 %reduce-scatter.25.cloned.1.call-done = bf16[128,768]{1,0:T(8,128)(2,1)} async-done(((bf16[4096,768]{1,0:T(8,128)(2,1)}), bf16[128,768]{1,0:T(8,128)(2,1)}) %reduce-scatter.25.cloned.1.call-update) | async-done | bytes 196624
  904.5 177.1 %reduce-scatter.27.cloned.1.call-done = bf16[128,768]{1,0:T(8,128)(2,1)} async-done(((bf16[4096,768]{1,0:T(8,128)(2,1)}), bf16[128,768]{1,0:T(8,128)(2,1)}) %reduce-scatter.27.cloned.1.call-update) | async-done | bytes 196624
  1088.8 18.3 %reduce-scatter.29.cloned.1.call-done = bf16[384,768]{1,0:T(8,128)(2,1)} async-done(((bf16[768,768]{1,0:T(8,128)(2,1)}), bf16[384,768]{1,0:T(8,128)(2,1)}) %reduce-scatter.29.cloned.1.call-update) | async-done | bytes 589840
  1108.4 26.9 %reduce-scatter.19.cloned.1.call-done = bf16[384,768]{1,0:T(8,128)(2,1)} async-done(((bf16[768,768]{1,0:T(8,128)(2,1)}), bf16[384,768]{1,0:T(8,128)(2,1)}) %reduce-scatter.19.cloned.1.call-update) | async-done | bytes 589840 | tf_op jit(solution)/shard_map/reduce_scatter | solution.py:244
  1135.4 66.3 %reduce-scatter.21.cloned.1.call-done = bf16[384,3072]{1,0:T(8,128)(2,1)} async-done(((bf16[768,3072]{1,0:T(8,128)(2,1)}), bf16[384,3072]{1,0:T(8,128)(2,1)}) %reduce-scatter.21.cloned.1.call-update) | async-done | bytes 2359312 | tf_op jit(solution)/shard_map/reduce_scatter | solution.py:262
  1201.7 66.6 %reduce-scatter.23.cloned.1.call-done = bf16[1536,768]{1,0:T(8,128)(2,1)} async-done(((bf16[3072,768]{1,0:T(8,128)(2,1)}), bf16[1536,768]{1,0:T(8,128)(2,1)}) %reduce-scatter.23.cloned.1.call-update) | async-done | bytes 2359312 | tf_op jit(solution)/shard_map/reduce_scatter | solution.py:268
  1281.7 14.6 reduce-scatter.31.cloned.1.call-done
  1297.7 26.8 %reduce-scatter.33.cloned.1.call-done = bf16[384,768]{1,0:T(8,128)(2,1)} async-done(((bf16[768,768]{1,0:T(8,128)(2,1)}), bf16[384,768]{1,0:T(8,128)(2,1)}) %reduce-scatter.33.cloned.1.call-update) | async-done | bytes 589840
  1325.9 356.2 %all-reduce.12 = (f32[384,768]{0,1:T(8,128)}, f32[384,768]{0,1:T(8,128)}, f32[384,768]{0,1:T(8,128)S(1)}, f32[384,768]{1,0:T(8,128)}, f32[384]{0:T(512)}, /*inde...) all-reduce(bf16[384,768]{0,1:T(8,128)(2,1)S(1)} %copy.69, ...), channel_id=1, replica_groups=mesh['ctx'=32,'seq'=2,'fsdp'=2] {'ctx','seq'}, use_global_device_ids=true, to_apply=%region_18.19 | all-reduce | flops 3543552 | bytes 21270528 | tf_op jit(solution)/shard_map/psum | solution.py:281
  (363 shorter events, 248.2 us)
Async XLA Ops:
  7.2 31.8 %all-gather.22.cloned.1.call-start = ((), (), s32[]{:S(2)}) async-start(), calls=%async_computation.11 | async-start | bytes 1769472 | tf_op jit(solution)/shard_map/all_gather | solution.py:97
  7.9 59.0 %all-gather.18.cloned.1.call-start = ((), (), s32[]{:S(2)}) async-start(), calls=%async_computation.9 | async-start | bytes 1769472 | tf_op jit(solution)/shard_map/all_gather | solution.py:98
  8.7 232.8 %all-gather.20.cloned.1.call-start = ((), (), s32[]{:S(2)}) async-start(), calls=%async_computation.10 | async-start | bytes 1769472 | tf_op jit(solution)/shard_map/all_gather | solution.py:96
  9.4 320.4 %all-gather.30.cloned.1.call-start = ((), (), s32[]{:S(2)}) async-start(), calls=%async_computation.18 | async-start | bytes 6488064 | tf_op jit(solution)/shard_map/all_gather | solution.py:111
  41.3 330.9 %all-gather.24.cloned.1.call-start = ((), (), s32[]{:S(2)}) async-start(), calls=%async_computation.12 | async-start | bytes 1769472 | tf_op jit(solution)/shard_map/all_gather | solution.py:99
  72.8 170.5 %all-to-all-start = ((bf16[32,1,128,768]{2,3,1,0:T(8,128)(2,1)}), bf16[32,1,128,768]{2,3,1,0:T(8,128)(2,1)}, u32[]{:S(2)}, u32[]{:S(2)}) async-start(bf16[32,1,128,768]{2,3,1,0:T(8,128)(2,1)} %stack.3), calls=%async_computation | async-start | bytes 12582912 | tf_op jit(solution)/shard_map/all_to_all | solution.py:14
  80.2 343.2 %all-gather.26.cloned.1.call-start = ((), (), s32[]{:S(2)}) async-start(), calls=%async_computation.13 | async-start | bytes 7077888 | tf_op jit(solution)/shard_map/all_gather | solution.py:135
  80.8 131.0 %copy-start.21 = (bf16[384]{0:T(512)(128)(2,1)S(1)}, bf16[384]{0:T(512)(128)(2,1)}, u32[]{:S(2)}) copy-start(bf16[384]{0:T(512)(128)(2,1)} %param.27) | copy-start | bytes 2308
  80.8 136.9 %copy-start.22 = (bf16[384]{0:T(512)(128)(2,1)S(1)}, bf16[384]{0:T(512)(128)(2,1)}, u32[]{:S(2)}) copy-start(bf16[384]{0:T(512)(128)(2,1)} %param.31) | copy-start | bytes 2308
  80.8 142.8 %copy-start.23 = (bf16[384]{0:T(512)(128)(2,1)S(1)}, bf16[384]{0:T(512)(128)(2,1)}, u32[]{:S(2)}) copy-start(bf16[384]{0:T(512)(128)(2,1)} %param.30) | copy-start | bytes 2308
  80.8 148.7 %copy-start.24 = (bf16[384]{0:T(512)(128)(2,1)S(1)}, bf16[384]{0:T(512)(128)(2,1)}, u32[]{:S(2)}) copy-start(bf16[384]{0:T(512)(128)(2,1)} %param.36) | copy-start | bytes 2308
  80.8 154.6 %copy-start.25 = (bf16[384]{0:T(512)(128)(2,1)S(1)}, bf16[384]{0:T(512)(128)(2,1)}, u32[]{:S(2)}) copy-start(bf16[384]{0:T(512)(128)(2,1)} %param.37) | copy-start | bytes 2308
  80.8 410.3 %all-gather.28.cloned.1.call-start = ((), (), s32[]{:S(2)}) async-start(), calls=%async_computation.14 | async-start | bytes 7077888 | tf_op jit(solution)/shard_map/all_gather | solution.py:137
  81.6 819.1 %reduce-scatter.25.cloned.1.call-start = ((), (), s32[]{:S(2)}) async-start(), calls=%async_computation.19 | async-start | bytes 6488064
  720.2 361.4 %reduce-scatter.27.cloned.1.call-start = ((), (), s32[]{:S(2)}) async-start(), calls=%async_computation.20 | async-start | bytes 6488064
  865.8 241.2 %reduce-scatter.29.cloned.1.call-start = ((), (), s32[]{:S(2)}) async-start(), calls=%async_computation.21 | async-start | bytes 1769472
  869.8 265.6 %reduce-scatter.19.cloned.1.call-start = ((), (), s32[]{:S(2)}) async-start(), calls=%async_computation.15 | async-start | bytes 1769472 | tf_op jit(solution)/shard_map/reduce_scatter | solution.py:244
  871.5 330.2 %reduce-scatter.21.cloned.1.call-start = ((), (), s32[]{:S(2)}) async-start(), calls=%async_computation.16 | async-start | bytes 7077888 | tf_op jit(solution)/shard_map/reduce_scatter | solution.py:262
  875.3 393.0 %reduce-scatter.23.cloned.1.call-start = ((), (), s32[]{:S(2)}) async-start(), calls=%async_computation.17 | async-start | bytes 7077888 | tf_op jit(solution)/shard_map/reduce_scatter | solution.py:268
  879.0 417.4 %reduce-scatter.31.cloned.1.call-start = ((), (), s32[]{:S(2)}) async-start(), calls=%async_computation.22 | async-start | bytes 1769472
  904.4 420.1 %reduce-scatter.33.cloned.1.call-start = ((), (), s32[]{:S(2)}) async-start(), calls=%async_computation.23 | async-start | bytes 1769472
  1087.5 191.1 %copy-start.1 = (bf16[768,768]{1,0:T(8,128)(2,1)S(1)}, bf16[768,768]{1,0:T(8,128)(2,1)}, u32[]{:S(2)}) copy-start(bf16[768,768]{1,0:T(8,128)(2,1)} %all-gather.22.cloned.1.call-done) | copy-start | bytes 3538948
  1088.8 191.6 %copy-start.2 = (bf16[768,768]{1,0:T(8,128)(2,1)S(1)}, bf16[768,768]{1,0:T(8,128)(2,1)}, u32[]{:S(2)}) copy-start(bf16[768,768]{1,0:T(8,128)(2,1)} %all-gather.18.cloned.1.call-done) | copy-start | bytes 3538948
  1088.8 191.7 %copy-start.8 = (bf16[6,1,128,128]{2,3,1,0:T(8,128)(2,1)S(1)}, bf16[6,1,128,128]{2,3,1,0:T(8,128)(2,1)}, u32[]{:S(2)}) copy-start(bf16[6,1,128,128]{2,3,1,0:T(8,128)(2,1)} %copy-done.7) | copy-start | bytes 589828
  (35 other events, 431.1 us)
Sparse Core Ops, SparseCore 0:
  9.7 29.2 all-gather.21
  40.6 26.2 all-gather.17
  68.6 38.4 all-gather.19
  109.2 220.6 all-gather.29
  331.3 24.2 all-gather.23
  357.1 66.1 all-gather.25
  425.0 66.1 all-gather.27
  720.4 180.2 reduce-scatter.24
  903.1 178.4 reduce-scatter.26
  1084.4 22.6 reduce-scatter.28
  1110.1 25.2 reduce-scatter.18
  1138.2 63.4 reduce-scatter.20
  1204.8 63.4 reduce-scatter.22
  1271.1 25.2 reduce-scatter.30
  1299.2 25.2 reduce-scatter.32
